TPU v7x, 32 devices: a whole 2x2x4 slice. The times are simulated.
32 devices in a mesh: slab: 4 (over x, core), dom: 8 (over z, y).
Axes of the slice: x: 2, y: 2, z: 4, core: 2. Of those that a mesh axis runs over, the one named last changes fastest.
Arguments:
- donors: bfloat16 [262144, 128], P(('slab', 'dom')), may hold values from -6 to 6
- send_block: int32 [4, 8, 8, 8], P('slab', 'dom'), may hold values from 0 to 63
- send_count: int32 [4, 8, 8], P('slab', 'dom'), may hold values from 1 to 8, as said below
- send_target: int32 [4, 8, 8, 8], P('slab', 'dom'), may hold values from 0 to 1
- target_block: int32 [4, 8, 8, 2], P('slab', 'dom'), may hold values from 0 to 7
- weights: bfloat16 [4, 8, 8, 8, 128, 128], P('slab', 'dom'), may hold values from -0.25 to 0.25
- halo_weights: bfloat16 [4, 8, 2, 128, 128], P('slab', 'dom'), may hold values from -0.375 to 0.375
- permute: int32 [4, 8, 1024], P('slab', 'dom'), may hold values from 0 to 1023, each once within a row
Outputs:
- balanced: bfloat16 [32768, 128], P(('slab', 'dom'))
Inputs may be any that keep to these rules, and one draw needn't show every extreme that they name: `send_count`: each source has at least one destination with exactly 8 live slots.
All inputs are finite; a program needn't handle non-finite values.
Results may differ from a plain program's by a relative error of at most 0.0047.
Values may be sent and summed in bfloat16 or wider, within the bound.
No kernel may reach another device: no remote copies, remote signals or barrier semaphores. Data moves between devices by JAX's collectives and lax.ppermute only.
A program may use at most 128 MiB of HBM per device.

v0:
```python
import jax
import jax.numpy as jnp
from jax import lax
from jax.sharding import PartitionSpec as P


def from_behind(value, axis, steps):
    count = lax.axis_size(axis)
    initial, last = (max(0, -steps), min(count, count - steps))
    return lax.ppermute(value, axis, [(source, source + steps) for source in range(initial, last)])


def on_device(
    donors, send_block, send_count, send_target, target_block, weights, halo_weights, permute
):
    hp = lax.Precision.HIGHEST
    block_rows = weights.shape[-1]
    width = donors.shape[1]
    blocks = donors.reshape(-1, block_rows, width)
    slots = send_block[0, 0]
    capacity = slots.shape[1]
    positions = target_block.shape[-1]
    live = jnp.arange(capacity)[None, :] < send_count[0, 0][:, None]
    choose = (send_target[0, 0][:, :, None] == jnp.arange(positions)[None, None, :]) & live[
        :, :, None
    ]
    picked = blocks[slots]
    local_weights = weights[0, 0]
    got_donors, got_weights, got_select = (
        lax.all_to_all(picked, "dom", split_axis=0, concat_axis=0, tiled=True),
        lax.all_to_all(local_weights, "dom", split_axis=0, concat_axis=0, tiled=True),
        lax.all_to_all(choose.astype(jnp.bfloat16), "dom", split_axis=0, concat_axis=0, tiled=True),
    )
    prods = jnp.einsum(
        "qcij,qcjv->qciv", got_weights, got_donors, preferred_element_type=jnp.float32
    )
    arrived = jnp.einsum(
        "qct,qciv->qtiv", got_select.astype(jnp.float32), prods, precision=hp
    ).astype(jnp.bfloat16)
    new_count = permute.shape[-1] // block_rows
    placer = (target_block[0, 0][:, :, None] == jnp.arange(new_count)[None, None, :]).astype(
        jnp.bfloat16
    )
    fresh = jnp.einsum("qtj,qtiv->jiv", placer, arrived, preferred_element_type=jnp.float32)
    rim_count = halo_weights.shape[2]
    rim = from_behind(blocks[blocks.shape[0] - rim_count :], "slab", 1)
    halo_term = jnp.einsum(
        "hij,hjv->iv", halo_weights[0, 0], rim, preferred_element_type=jnp.float32
    )
    fresh = fresh.at[0].add(halo_term)
    new_rows = fresh.astype(jnp.bfloat16).reshape(-1, width)
    ordered = new_rows[permute[0, 0]]
    return lax.all_to_all(ordered, "dom", split_axis=0, concat_axis=0, tiled=True)


def solution(mesh):
    return jax.shard_map(
        on_device,
        mesh=mesh,
        in_specs=(
            P(("slab", "dom"), None),
            P("slab", "dom", None, None),
            P("slab", "dom", None),
            P("slab", "dom", None, None),
            P("slab", "dom", None, None),
            P("slab", "dom", None, None, None, None),
            P("slab", "dom", None, None, None),
            P("slab", "dom", None),
        ),
        out_specs=P(("slab", "dom"), None),
        check_vma=False,
    )
```

profile of v0, /device:TPU:0, one launch (start us, length us, event | category | flops | bytes accessed | tf_op | source)
XLA Modules:
  0.0 152.3 jit_solution(8960431171635038401)
XLA Ops:
  0.0 0.7 compare_select_fusion.1
  0.7 0.1 reshape.129
  0.8 2.5 %gather_fusion = bf16[64,128,128]{2,1,0:T(8,128)(2,1)S(1)} fusion(bf16[64,128,128]{2,1,0:T(8,128)(2,1)} %bitcast.41, s32[1024]{0:T(1024)S(1)} %pad_clamp_fusion), kind=kCustom, calls=%fused_computation | custom fusion | bytes 4194560 | tf_op jit(solution)/shard_map/gather | solution.py:27
  3.4 2.9 %copy.13 = bf16[64,128,128]{1,2,0:T(8,128)(2,1)} copy(bf16[64,128,128]{2,1,0:T(8,128)(2,1)S(1)} %gather_fusion) | data formatting | bytes 4194304 | tf_op jit(solution)/shard_map/gather | solution.py:27
  6.3 55.5 %all_to_all.27 = bf16[8,8,128,128]{2,3,1,0:T(8,128)(2,1)S(1)} all-to-all(bf16[8,8,128,128]{2,3,1,0:T(8,128)(2,1)} %bitcast.40), channel_id=1, replica_groups=mesh['slab'=4,'dom'=8] {'dom'}, dimensions={0} | all-to-all | bytes 4194304 | tf_op jit(solution)/shard_map/all_to_all | solution.py:30
  61.8 4.5 %all-to-all-start.2 = ((bf16[8,8,128,128]{3,2,1,0:T(8,128)(2,1)}), bf16[8,8,128,128]{3,2,1,0:T(8,128)(2,1)}, u32[]{:S(2)}, u32[]{:S(2)}) async-start(bf16[8,8,128,128]{3,2,1,0:T(8,128)(2,1)} %bitcast.42), calls=%async_computation.2 | async-start | bytes 4194304 | tf_op jit(solution)/shard_map/all_to_all | solution.py:31
  66.3 0.8 slice.29
  67.2 1.3 collective-permute-start
  68.5 0.1 iota_compare_fusion.1
  68.6 0.6 and_convert_fusion
  69.2 0.2 collective-permute-done
  69.3 0.1 fusion.1
  69.5 44.2 %all-to-all-done.2 = bf16[8,8,128,128]{3,2,1,0:T(8,128)(2,1)} async-done(((bf16[8,8,128,128]{3,2,1,0:T(8,128)(2,1)}), bf16[8,8,128,128]{3,2,1,0:T(8,128)(2,1)}, u32[]{:S(2)}, u32[]{:S(2)}) %all-to-all-start.2) | async-done | bytes 2097184 | tf_op jit(solution)/shard_map/all_to_all | solution.py:31
  113.6 3.6 %all-to-all-start = ((bf16[8,8,2]{1,2,0:T(2,128)(2,1)}), bf16[8,8,2]{1,2,0:T(2,128)(2,1)S(1)}, u32[]{:S(2)}, u32[]{:S(2)}) async-start(bf16[8,8,2]{1,2,0:T(2,128)(2,1)} %and_convert_fusion), calls=%async_computation | async-start | bytes 8192 | tf_op jit(solution)/shard_map/all_to_all | solution.py:32
  117.3 5.1 %convolution_bitcast_fusion = f32[8,8,128,128]{2,3,1,0:T(8,128)} fusion(bf16[8,8,128,128]{2,3,1,0:T(8,128)(2,1)S(1)} %all_to_all.27, bf16[8,8,128,128]{3,2,1,0:T(8,128)(2,1)} %all-to-all-done.2), kind=kOutput, calls=%fused_computation.2 | convolution fusion | flops 268435456 | bytes 8388608 | tf_op jit(solution)/shard_map/qcij,qcjv->qciv/dot_general | solution.py:34
  122.4 5.4 %copy.14 = f32[8,8,128,128]{3,1,2,0:T(8,128)} copy(f32[8,8,128,128]{2,3,1,0:T(8,128)} %convolution_bitcast_fusion) | data formatting | bytes 8388608 | tf_op jit(solution)/shard_map/qcij,qcjv->qciv/dot_general | solution.py:34
  127.7 0.0 all-to-all-done
  127.7 4.3 %convolution_convert_fusion = bf16[8,2,128,128]{3,1,2,0:T(2,128)(2,1)S(1)} fusion(f32[8,8,128,128]{3,1,2,0:T(8,128)} %copy.14, bf16[8,8,2]{1,2,0:T(2,128)(2,1)S(1)} %all-to-all-done), kind=kOutput, calls=%fused_computation.3 | convolution fusion | flops 25427968 | bytes 4718848 | tf_op jit(solution)/shard_map/qct,qciv->qtiv/dot_general | solution.py:37
  132.1 0.4 convolution_bitcast_fusion.1
  132.5 0.1 slice_add_fusion
  132.5 1.4 scatter-add.4
  134.1 3.2 %gather_fusion.1 = bf16[1024,128]{1,0:T(8,128)(2,1)S(1)} fusion(bf16[1024,128]{1,0:T(8,128)(2,1)S(1)} %bitcast.39, s32[1024]{0:T(1024)S(1)} %broadcast_clamp_fusion), kind=kCustom, calls=%fused_computation.1 | custom fusion | bytes 528384 | tf_op jit(solution)/shard_map/gather | solution.py:52
  137.3 14.3 %all_to_all.28 = bf16[8,128,128]{2,1,0:T(8,128)(2,1)S(1)} all-to-all(bf16[8,128,128]{2,1,0:T(8,128)(2,1)S(1)} %bitcast.43), channel_id=1, replica_groups=mesh['slab'=4,'dom'=8] {'dom'}, dimensions={0} | all-to-all | bytes 524288 | tf_op jit(solution)/shard_map/all_to_all | solution.py:53
  151.6 0.7 copy.23
  (15 shorter events, 0.1 us)
Async XLA Ops:
  0.0 69.3 %copy-start = (bf16[1,1,2,128,128]{4,3,2,1,0:T(8,128)(2,1)S(1)}, bf16[1,1,2,128,128]{4,3,2,1,0:T(8,128)(2,1)}, u32[]{:S(2)}) copy-start(bf16[1,1,2,128,128]{4,3,2,1,0:T(8,128)(2,1)} %param.16) | copy-start | bytes 196612
  61.8 6.6 %copy-start.4 = (s32[1,1,8]{2,1,0:T(1,128)S(1)}, s32[1,1,8]{2,1,0:T(1,128)}, u32[]{:S(2)}) copy-start(s32[1,1,8]{2,1,0:T(1,128)} %param.12) | copy-start | bytes 100
  61.8 6.7 %copy-start.1 = (s32[1,1,1024]{2,1,0:T(1,128)S(1)}, s32[1,1,1024]{2,1,0:T(1,128)}, u32[]{:S(2)}) copy-start(s32[1,1,1024]{2,1,0:T(1,128)} %param.17) | copy-start | bytes 12292
  61.8 6.7 %copy-start.2 = (s32[1,1,8,8]{3,2,1,0:T(8,128)S(1)}, s32[1,1,8,8]{3,2,1,0:T(8,128)}, u32[]{:S(2)}) copy-start(s32[1,1,8,8]{3,2,1,0:T(8,128)} %param.13) | copy-start | bytes 772
  61.8 51.8 %all-to-all-start.2 = ((bf16[8,8,128,128]{3,2,1,0:T(8,128)(2,1)}), bf16[8,8,128,128]{3,2,1,0:T(8,128)(2,1)}, u32[]{:S(2)}, u32[]{:S(2)}) async-start(bf16[8,8,128,128]{3,2,1,0:T(8,128)(2,1)} %bitcast.42), calls=%async_computation.2 | async-start | bytes 4194304 | tf_op jit(solution)/shard_map/all_to_all | solution.py:31
  67.2 2.2 %collective-permute-start = (bf16[2,128,128]{2,1,0:T(8,128)(2,1)S(1)}, bf16[2,128,128]{2,1,0:T(8,128)(2,1)S(1)}, u32[]{:S(2)}, u32[]{:S(2)}) collective-permute-start(bf16[2,128,128]{2,1,0:T(8,128)(2,1)S(1)} %bitcast.46), channel_id=1, source_target_pairs={{0,8},{8,16},{16,24},{1,9},{9,17},{17,25},{2,10},{10,18},{18,26},{... | collective-permute-start | bytes 196616 | tf_op jit(solution)/shard_map/ppermute | solution.py:10
  113.6 14.1 %all-to-all-start = ((bf16[8,8,2]{1,2,0:T(2,128)(2,1)}), bf16[8,8,2]{1,2,0:T(2,128)(2,1)S(1)}, u32[]{:S(2)}, u32[]{:S(2)}) async-start(bf16[8,8,2]{1,2,0:T(2,128)(2,1)} %and_convert_fusion), calls=%async_computation | async-start | bytes 8192 | tf_op jit(solution)/shard_map/all_to_all | solution.py:32
  127.7 4.3 %copy-start.3 = (s32[1,1,8,2]{2,3,1,0:T(2,128)S(1)}, s32[1,1,8,2]{2,3,1,0:T(2,128)}, u32[]{:S(2)}) copy-start(s32[1,1,8,2]{2,3,1,0:T(2,128)} %param.14) | copy-start | bytes 196
where the time goes:
time: 153 us; the launch traced here: 152 us
  blocking collectives  69.9 us (46%)
  waiting for transfers between devices  44.3 us (29%)
  local copies, waits for them, and re-layouts  17.2 us (11%)
  matrix products  9.96 us (7%)
  starting transfers between devices  9.38 us (6%)
    all_to_all x1, blocking collectives, on_device(): lax.all_to_all(picked, 'dom', split_axis=0, concat_axis=0, tiled=True)  55.5 us
    all_to_all x1, waiting for transfers between devices, on_device(): lax.all_to_all(local_weights, 'dom', split_axis=0, concat_axis=0, tiled=T...  44.2 us
    all_to_all x1, blocking collectives, on_device(): lax.all_to_all(ordered, 'dom', split_axis=0, concat_axis=0, tiled=True)  14.3 us
    gather x2, local copies, waits for them, and re-layouts, on_device(): picked = blocks[slots]  5.45 us
    dot_general x1, local copies, waits for them, and re-layouts, on_device(): jnp.einsum('qcij,qcjv->qciv', got_weights, got_donors, preferred_element_...  5.38 us
    dot_general x1, matrix products, on_device(): jnp.einsum('qcij,qcjv->qciv', got_weights, got_donors, preferred_element_...  5.1 us
    all_to_all x1, starting transfers between devices, on_device(): lax.all_to_all(local_weights, 'dom', split_axis=0, concat_axis=0, tiled=T...  4.48 us
    dot_general x1, matrix products, on_device(): jnp.einsum('qct,qciv->qtiv', got_select.astype(jnp.float32), prods, preci...  4.31 us
  transfers between devices with their start and end apart: 3, of which 2 were waited for; matrix products, arithmetic and copies ran while one was open for 8% of the time, Pallas kernels for 0%

commit v1 on v0

v1 whole, which is shorter than its diff:
```python
import jax
import jax.numpy as jnp
from jax import lax
from jax.experimental import pallas as pl
from jax.experimental.pallas import tpu as pltpu
from jax.sharding import PartitionSpec as P


def parts_kernel(block_of, count_of, target_of, donors, weights, out, held_w, held_d, sem_w, sem_d):
    n_dest, capacity = block_of.shape
    rows = held_w.shape[2]
    places = out.shape[1]

    def start(p, carry):
        pltpu.make_async_copy(weights.at[p], held_w.at[p], sem_w.at[p]).start()
        for c in range(capacity):
            row = pl.multiple_of(block_of[p, c] * rows, rows)
            pltpu.make_async_copy(
                donors.at[pl.ds(row, rows)], held_d.at[p, pl.ds(c * rows, rows)], sem_d.at[p]
            ).start()
        return carry

    lax.fori_loop(0, n_dest, start, 0)

    def work(p, carry):
        pltpu.make_async_copy(weights.at[p], held_w.at[p], sem_w.at[p]).wait()
        pltpu.make_async_copy(held_d.at[p], held_d.at[p], sem_d.at[p]).wait()
        total = None
        for c in range(0, capacity, 2):
            left = jnp.concatenate([held_w[p, c], held_w[p, c + 1]], axis=1)
            pieces = []
            for k in (c, c + 1):
                block = held_d[p, pl.ds(k * rows, rows)]
                live = k < count_of[p]
                kept = []
                for t in range(places):
                    wanted = jnp.logical_and(live, target_of[p, k] == t)
                    kept.append(jnp.where(wanted, block, jnp.zeros_like(block)))
                pieces.append(jnp.concatenate(kept, axis=1))
            right = jnp.concatenate(pieces, axis=0)
            prod = jnp.dot(left, right, preferred_element_type=jnp.float32)
            total = prod if total is None else total + prod
        width = out.shape[-1]
        for t in range(places):
            out[p, t] = total[:, t * width : (t + 1) * width].astype(out.dtype)
        return carry

    lax.fori_loop(0, n_dest, work, 0)


def form_parts(slots, counts, targets, donors, weights, places):
    n_dest, capacity, rows, _ = weights.shape
    width = donors.shape[1]
    smem = pl.BlockSpec(memory_space=pltpu.SMEM)
    hbm = pl.BlockSpec(memory_space=pl.ANY)
    return pl.pallas_call(
        parts_kernel,
        out_shape=jax.ShapeDtypeStruct((n_dest, places, rows, width), jnp.bfloat16),
        in_specs=[smem, smem, smem, hbm, hbm],
        out_specs=pl.BlockSpec(memory_space=pltpu.VMEM),
        scratch_shapes=[
            pltpu.VMEM((n_dest, capacity, rows, rows), weights.dtype),
            pltpu.VMEM((n_dest, capacity * rows, width), donors.dtype),
            pltpu.SemaphoreType.DMA((n_dest,)),
            pltpu.SemaphoreType.DMA((n_dest,)),
        ],
        name="parts",
    )(slots, counts, targets, donors, weights)


def place_kernel(place_of, parts, halo_w, rim, order, out, fresh):
    n_src, places = place_of.shape
    rows, width = parts.shape[2:]
    total_rows = fresh.shape[0]
    halo = jnp.zeros((rows, width), jnp.float32)
    for h in range(halo_w.shape[0]):
        halo += jnp.dot(halo_w[h], rim[h], preferred_element_type=jnp.float32)
    fresh[pl.ds(0, rows)] = halo
    fresh[pl.ds(rows, total_rows - rows)] = jnp.zeros((total_rows - rows, width), jnp.float32)

    def add(q, carry):
        for t in range(places):
            row = pl.multiple_of(place_of[q, t] * rows, rows)
            fresh[pl.ds(row, rows)] += parts[q, t].astype(jnp.float32)
        return carry

    lax.fori_loop(0, n_src, add, 0)
    values = fresh[...].astype(jnp.bfloat16)
    lane = lax.broadcasted_iota(jnp.int32, (rows, total_rows), 1)

    def pick(j, carry):
        wanted = jnp.broadcast_to(order[pl.ds(j, 1), :], (rows, rows)).T
        wanted = jnp.concatenate([wanted] * (total_rows // rows), axis=1)
        chosen = jnp.where(lane == wanted, 1.0, 0.0).astype(jnp.bfloat16)
        row = pl.multiple_of(j * rows, rows)
        out[pl.ds(row, rows)] = jnp.dot(
            chosen, values, preferred_element_type=jnp.float32
        ).astype(out.dtype)
        return carry

    lax.fori_loop(0, total_rows // rows, pick, 0)


def place_parts(places_of, parts, halo_w, rim, order):
    rows, width = parts.shape[2:]
    total_rows = order.size
    smem = pl.BlockSpec(memory_space=pltpu.SMEM)
    vmem = pl.BlockSpec(memory_space=pltpu.VMEM)
    return pl.pallas_call(
        place_kernel,
        out_shape=jax.ShapeDtypeStruct((total_rows, width), jnp.bfloat16),
        in_specs=[smem, vmem, vmem, vmem, vmem],
        out_specs=vmem,
        scratch_shapes=[pltpu.VMEM((total_rows, width), jnp.float32)],
        name="place",
    )(places_of, parts, halo_w, rim, order)


def on_device(
    donors, send_block, send_count, send_target, target_block, weights, halo_weights, permute
):
    block_rows = weights.shape[-1]
    width = donors.shape[1]
    rim_count = halo_weights.shape[2]
    slabs = lax.axis_size("slab")
    rim = lax.ppermute(
        donors[donors.shape[0] - rim_count * block_rows :].reshape(rim_count, block_rows, width),
        "slab",
        [(source, source + 1) for source in range(slabs - 1)],
    )
    parts = form_parts(
        send_block[0, 0], send_count[0, 0], send_target[0, 0], donors, weights[0, 0],
        target_block.shape[-1],
    )
    arrived = lax.all_to_all(parts, "dom", split_axis=0, concat_axis=0, tiled=True)
    ordered = place_parts(
        target_block[0, 0], arrived, halo_weights[0, 0], rim, permute[0, 0].reshape(-1, block_rows)
    )
    return lax.all_to_all(ordered, "dom", split_axis=0, concat_axis=0, tiled=True)


def solution(mesh):
    return jax.shard_map(
        on_device,
        mesh=mesh,
        in_specs=(
            P(("slab", "dom"), None),
            P("slab", "dom", None, None),
            P("slab", "dom", None),
            P("slab", "dom", None, None),
            P("slab", "dom", None, None),
            P("slab", "dom", None, None, None, None),
            P("slab", "dom", None, None, None),
            P("slab", "dom", None),
        ),
        out_specs=P(("slab", "dom"), None),
        check_vma=False,
    )
```

time: 153 us -> 45.9 us (0.30)
  blocking collectives: 69.9 us -> 12.7 us
  waiting for transfers between devices: 44.3 us -> 11.5 us
  local copies, waits for them, and re-layouts: 17.2 us -> 3 us
  matrix products: 9.96 us -> 0 us
  Pallas kernels: 0 us -> 9.34 us
    all_to_all x1 -> x0, blocking collectives: 55.5 us -> none  [on_device(): lax.all_to_all(picked, 'dom', split_axis=0, concat_axis=0, tiled=True)]
    all_to_all x2 -> x1, waiting for transfers between devices: 44.2 us -> 11.3 us  [on_device(): lax.all_to_all(parts, 'dom', split_axis=0, concat_axis=0, tiled=True)]
    dot_general x4 -> x0, matrix products: 9.96 us -> none  [the longest x1 5.1 us: on_device(): jnp.einsum('qcij,qcjv->qciv', got_weights, got_donors, preferred_element_...]
    pallas_call x0 -> x2, Pallas kernels: none -> 9.34 us  [the longest x1 4.97 us: form_parts(): pl.pallas_call(parts_kernel, out_shape=jax.ShapeDtypeStruct((n_dest, plac...]
    gather x3 -> x0, local copies, waits for them, and re-layouts: 8.66 us -> none  [the longest x2 5.45 us: on_device(): picked = blocks[slots]]
    dot_general x1 -> x0, local copies, waits for them, and re-layouts: 5.38 us -> none  [on_device(): jnp.einsum('qcij,qcjv->qciv', got_weights, got_donors, preferred_element_...]
    all_to_all x1, blocking collectives: 14.3 us -> 12.7 us  [on_device(): lax.all_to_all(ordered, 'dom', split_axis=0, concat_axis=0, tiled=True)]
    all_to_all x2 -> x1, starting transfers between devices: 8.1 us -> 7.45 us  [on_device(): lax.all_to_all(parts, 'dom', split_axis=0, concat_axis=0, tiled=True)]
  transfers between devices with their start and end apart: 3 -> 2, of which waited for: 2 -> 2; matrix products, arithmetic and copies ran while one was open for 8% -> 3% of each run, Pallas kernels for 0% -> 0%
where the time goes in v1:
time: 45.9 us; the launch traced here: 45.5 us
  blocking collectives  12.7 us (28%)
  waiting for transfers between devices  11.5 us (25%)
  Pallas kernels  9.34 us (20%)
  starting transfers between devices  8.86 us (19%)
  local copies, waits for them, and re-layouts  3 us (7%)
    all_to_all x1, blocking collectives, on_device(): lax.all_to_all(ordered, 'dom', split_axis=0, concat_axis=0, tiled=True)  12.7 us
    all_to_all x1, waiting for transfers between devices, on_device(): lax.all_to_all(parts, 'dom', split_axis=0, concat_axis=0, tiled=True)  11.3 us
    all_to_all x1, starting transfers between devices, on_device(): lax.all_to_all(parts, 'dom', split_axis=0, concat_axis=0, tiled=True)  7.45 us
    pallas_call x1, Pallas kernels, form_parts(): pl.pallas_call(parts_kernel, out_shape=jax.ShapeDtypeStruct((n_dest, plac...  4.97 us
    pallas_call x1, Pallas kernels, place_parts(): pl.pallas_call(place_kernel, out_shape=jax.ShapeDtypeStruct((total_rows,...  4.37 us
    unnamed x7, local copies, waits for them, and re-layouts  1.49 us
    ppermute x1, starting transfers between devices, on_device(): lax.ppermute(donors[donors.shape[0] - rim_count * block_rows:].reshape(ri...  1.41 us
  transfers between devices with their start and end apart: 2, of which 2 were waited for; matrix products, arithmetic and copies ran while one was open for 3% of the time, Pallas kernels for 0%

profile of v1, /device:TPU:0, one launch (start us, length us, event | category | flops | bytes accessed | tf_op | source)
XLA Modules:
  0.0 45.5 jit_solution(8323007057794555290)
XLA Ops:
  0.0 0.0 copy-start.2
  0.0 5.0 %parts.1 = bf16[8,2,128,128]{3,2,1,0:T(8,128)(2,1)} custom-call(s32[8,8]{1,0:T(8,128)} %bitcast.15, s32[8]{0:T(128)} %bitcast.19, s32[8,8]{1,0:T(8,128)} %bitcast.16, bf16[8192,128]{1,0:T(8,128)(2,1)} %donors.1, bf16[8,8,128,128]{3,2,1,0:T(8,128)(2,1)} %bitcast.10), custom_call_target="tpu_custom_call" | custom-call | tf_op jit(solution)/shard_map/parts/pallas_call | solution.py:56
  5.0 7.4 %all-to-all-start = ((bf16[8,2,128,128]{3,2,1,0:T(8,128)(2,1)}), bf16[8,2,128,128]{3,2,1,0:T(8,128)(2,1)S(1)}, u32[]{:S(2)}, u32[]{:S(2)}) async-start(bf16[8,2,128,128]{3,2,1,0:T(8,128)(2,1)} %parts.1), calls=%async_computation | async-start | bytes 1048576 | tf_op jit(solution)/shard_map/all_to_all | solution.py:135
  12.4 0.8 %slice.3 = bf16[256,128]{1,0:T(8,128)(2,1)S(1)} slice(bf16[8192,128]{1,0:T(8,128)(2,1)} %donors.1), slice={[7936:8192], [0:128]} | slice | bytes 131072 | tf_op jit(solution)/shard_map/slice | solution.py:127
  13.3 1.4 %collective-permute-start = (bf16[2,128,128]{2,1,0:T(8,128)(2,1)S(1)}, bf16[2,128,128]{2,1,0:T(8,128)(2,1)S(1)}, u32[]{:S(2)}, u32[]{:S(2)}) collective-permute-start(bf16[2,128,128]{2,1,0:T(8,128)(2,1)S(1)} %bitcast.14), channel_id=1, source_target_pairs={{0,8},{8,16},{16,24},{1,9},{9,17},{17,25},{2,10},{10,18},{18,26},{... | collective-permute-start | bytes 196616 | tf_op jit(solution)/shard_map/ppermute | solution.py:126
  14.7 0.0 copy-done.2
  14.7 0.7 %copy.9.place_of = s32[8,2]{1,0:T(8,128)} copy(s32[8,2]{0,1:T(2,128)S(1)} %bitcast.18) | data formatting | bytes 128 | tf_op jit(solution)/shard_map/squeeze | solution.py:137
  15.4 0.2 collective-permute-done.rim
  15.6 0.0 copy-start.1
  15.6 11.3 %all-to-all-done.parts = bf16[8,2,128,128]{3,2,1,0:T(8,128)(2,1)S(1)} async-done(((bf16[8,2,128,128]{3,2,1,0:T(8,128)(2,1)}), bf16[8,2,128,128]{3,2,1,0:T(8,128)(2,1)S(1)}, u32[]{:S(2)}, u32[]{:S(2)}) %all-to-all-start) | async-done | bytes 524320 | tf_op jit(solution)/shard_map/all_to_all | solution.py:135
  26.9 0.0 copy-start
  26.9 0.0 copy-done.1
  26.9 0.8 %copy-done = bf16[8,2,128,128]{3,2,1,0:T(8,128)(2,1)} copy-done((bf16[8,2,128,128]{3,2,1,0:T(8,128)(2,1)}, bf16[8,2,128,128]{3,2,1,0:T(8,128)(2,1)S(1)}, u32[]{:S(2)}) %copy-start) | copy-done | bytes 524312
  27.7 4.4 %place.1 = bf16[1024,128]{1,0:T(8,128)(2,1)} custom-call(s32[8,2]{1,0:T(8,128)} %copy.9.place_of, bf16[8,2,128,128]{3,2,1,0:T(8,128)(2,1)} %copy-done, bf16[2,128,128]{2,1,0:T(8,128)(2,1)} %bitcast.13, bf16[2,128,128]{2,1,0:T(8,128)(2,1)} %copy-done.1, s32[8,128]{1,0:T(8,128)} %bitcast.17), custom_call_target="tpu_custom_call" | custom-call | tf_op jit(solution)/shard_map/place/pallas_call | solution.py:109
  32.0 12.7 %all_to_all.17 = bf16[8,128,128]{2,1,0:T(8,128)(2,1)S(1)} all-to-all(bf16[8,128,128]{2,1,0:T(8,128)(2,1)} %bitcast.11), channel_id=1, replica_groups=mesh['slab'=4,'dom'=8] {'dom'}, dimensions={0} | all-to-all | bytes 524288 | tf_op jit(solution)/shard_map/all_to_all | solution.py:139
  44.8 0.7 %copy.11 = bf16[1024,128]{1,0:T(8,128)(2,1)} copy(bf16[1024,128]{1,0:T(8,128)(2,1)S(1)} %bitcast.12) | data formatting | bytes 524288
Async XLA Ops:
  0.0 14.7 %copy-start.2 = (s32[1,1,8,2]{2,3,1,0:T(2,128)S(1)}, s32[1,1,8,2]{2,3,1,0:T(2,128)}, u32[]{:S(2)}) copy-start(s32[1,1,8,2]{2,3,1,0:T(2,128)} %param.12) | copy-start | bytes 196
  5.0 21.9 %all-to-all-start = ((bf16[8,2,128,128]{3,2,1,0:T(8,128)(2,1)}), bf16[8,2,128,128]{3,2,1,0:T(8,128)(2,1)S(1)}, u32[]{:S(2)}, u32[]{:S(2)}) async-start(bf16[8,2,128,128]{3,2,1,0:T(8,128)(2,1)} %parts.1), calls=%async_computation | async-start | bytes 1048576 | tf_op jit(solution)/shard_map/all_to_all | solution.py:135
  13.3 2.3 %collective-permute-start = (bf16[2,128,128]{2,1,0:T(8,128)(2,1)S(1)}, bf16[2,128,128]{2,1,0:T(8,128)(2,1)S(1)}, u32[]{:S(2)}, u32[]{:S(2)}) collective-permute-start(bf16[2,128,128]{2,1,0:T(8,128)(2,1)S(1)} %bitcast.14), channel_id=1, source_target_pairs={{0,8},{8,16},{16,24},{1,9},{9,17},{17,25},{2,10},{10,18},{18,26},{... | collective-permute-start | bytes 196616 | tf_op jit(solution)/shard_map/ppermute | solution.py:126
  15.6 11.3 %copy-start.1 = (bf16[2,128,128]{2,1,0:T(8,128)(2,1)}, bf16[2,128,128]{2,1,0:T(8,128)(2,1)S(1)}, u32[]{:S(2)}) copy-start(bf16[2,128,128]{2,1,0:T(8,128)(2,1)S(1)} %collective-permute-done.rim) | copy-start | bytes 196612
  26.9 0.8 %copy-start = (bf16[8,2,128,128]{3,2,1,0:T(8,128)(2,1)}, bf16[8,2,128,128]{3,2,1,0:T(8,128)(2,1)S(1)}, u32[]{:S(2)}) copy-start(bf16[8,2,128,128]{3,2,1,0:T(8,128)(2,1)S(1)} %all-to-all-done.parts) | copy-start | bytes 1572868
